TPU v7x, 32 devices: a whole 2x2x4 slice. The times are simulated.
32 devices in a mesh: grp: 2 (over y), blk: 4 (over z), head: 2 (over x), sub: 2 (over core).
Axes of the slice: x: 2, y: 2, z: 4, core: 2. Of those that a mesh axis runs over, the one named last changes fastest.
Arguments:
- queries: bfloat16 [4096, 4096], P(('grp', 'blk', 'head', 'sub')), parts along dimension 0, may hold values from -46 to 46
- keys: bfloat16 [4096, 4096], P(('grp', 'blk', 'head', 'sub')), parts along dimension 0, may hold values from -4 to 4
- values: bfloat16 [4096, 4096], P(('grp', 'blk', 'head', 'sub')), parts along dimension 0, may hold values from -6 to 6
- block_lists: int32 [32, 16, 8], replicated, may hold values from 0 to 15, as said below
Outputs:
- attended: bfloat16 [4096, 4096], P(('grp', 'blk', 'head', 'sub')), parts along dimension 0
There are 2 independent parts, one for each index of `grp`. A program takes and returns all parts, laid end to end along the dimension named above; an argument that names none is the same for every part. Nothing has to cross between parts.
Inputs may be any that keep to these rules, and one draw needn't show every extreme that they name: `block_lists`: the first entry of every list is the query tile itself; entries may repeat. Tiles are numbered frame by frame, 4 to a frame. In each head either all entries lie in the query tile's frame or the frames next to it, or all entries have the query tile's position within its frame.
All inputs are finite; a program needn't handle non-finite values.
Results may differ from a plain program's by a relative error of at most 0.0065.
Values may be sent and summed in bfloat16 or wider, within the bound.
A program may use at most 64 MiB of HBM per device.

v0:
```python
import math

import jax
import jax.numpy as jnp
from jax import lax
from jax.sharding import PartitionSpec as P

HEADS = 32
HEAD_DIM = 128
TILE = 128


NEG_FLOOR = -1e30


def query_rows(block_lists, first_head, heads_here, query_tokens):
    tile_ids = jnp.arange(block_lists.shape[1], dtype=jnp.int32)
    lists_local = lax.dynamic_slice_in_dim(block_lists, first_head, heads_here, 0)
    tile_mask = jnp.any(lists_local[:, :, :, None] == tile_ids, axis=2).astype(jnp.bfloat16)
    query_onehot = ((query_tokens // TILE)[:, None] == tile_ids[None, :]).astype(jnp.bfloat16)
    listed = jnp.einsum("qi,hij->hqj", query_onehot, tile_mask, preferred_element_type=jnp.float32)
    return listed.astype(jnp.bfloat16)


def attend_block(state_now, key_block, value_block, allowed, query_local, score_scale):
    top_old, total_old, accum_old = state_now
    scores = (
        jnp.einsum("qhd,khd->hqk", query_local, key_block, preferred_element_type=jnp.float32)
        * score_scale
    )
    top_new = jnp.maximum(top_old, jnp.max(jnp.where(allowed, scores, NEG_FLOOR), axis=2))
    factor = jnp.exp(top_old - top_new)
    weights = jnp.where(allowed, jnp.exp(scores - top_new[:, :, None]), 0.0)
    total_new = total_old * factor + jnp.sum(weights, axis=2)
    product = jnp.einsum(
        "hqk,khd->qhd",
        weights.astype(jnp.bfloat16),
        value_block,
        preferred_element_type=jnp.float32,
    )
    accum_new = accum_old * jnp.transpose(factor)[:, :, None] + product
    return (top_new, total_new, accum_new)


def make_step(query_local, listed_rows, key_token, block_len, tile_total):
    score_scale = 1.0 / math.sqrt(HEAD_DIM)
    tile_ids = jnp.arange(tile_total, dtype=jnp.int32)

    def fold_step(state_now, piece, first_row):
        key_piece, value_piece = piece
        block_count = key_piece.shape[0] // block_len

        def one_block(block_index, state_in):
            key_block = lax.dynamic_slice_in_dim(key_piece, block_index * block_len, block_len, 0)
            value_block = lax.dynamic_slice_in_dim(
                value_piece, block_index * block_len, block_len, 0
            )
            positions = block_index * block_len + jnp.arange(block_len, dtype=jnp.int32)
            key_tiles = key_token(positions) // TILE
            key_onehot = (tile_ids[:, None] == key_tiles[None, :]).astype(jnp.bfloat16)
            allowed = (
                jnp.einsum(
                    "hqj,jk->hqk", listed_rows, key_onehot, preferred_element_type=jnp.float32
                )
                > 0.5
            )
            result = attend_block(
                state_in, key_block, value_block, allowed, query_local, score_scale
            )
            return result

        return lax.fori_loop(0, block_count, one_block, state_now)

    return fold_step


def start_state(heads_here, block_len):
    top_all = jnp.full((heads_here, block_len), NEG_FLOOR, jnp.float32)
    total_all = jnp.zeros((heads_here, block_len), jnp.float32)
    accum_all = jnp.zeros((block_len, heads_here, HEAD_DIM), jnp.float32)
    return (top_all, total_all, accum_all)


def normalize(state_end):
    top_all, total_all, accum_all = state_end
    return (accum_all / jnp.transpose(total_all)[:, :, None]).astype(jnp.bfloat16)


def per_device(queries, keys, values, block_lists):
    row_count, col_count = queries.shape
    n_head = lax.axis_size("head")
    n_sub = lax.axis_size("sub")
    blk_index = lax.axis_index("blk")
    head_index = lax.axis_index("head")
    sub_index = lax.axis_index("sub")
    tile_total = block_lists.shape[1]
    heads_here = HEADS // (n_head * n_sub)
    block_len = row_count * n_head * n_sub

    def inward(tensor):
        return tensor.reshape(1, 1, row_count, n_head, n_sub, heads_here * HEAD_DIM)

    query_six, keys_six, values_six = (
        lax.all_to_all(
            lax.all_to_all(inward(queries), "head", split_axis=3, concat_axis=1, tiled=True),
            "sub",
            split_axis=4,
            concat_axis=0,
            tiled=True,
        ),
        lax.all_to_all(
            lax.all_to_all(inward(keys), "head", split_axis=3, concat_axis=1, tiled=True),
            "sub",
            split_axis=4,
            concat_axis=0,
            tiled=True,
        ),
        lax.all_to_all(
            lax.all_to_all(inward(values), "head", split_axis=3, concat_axis=1, tiled=True),
            "sub",
            split_axis=4,
            concat_axis=0,
            tiled=True,
        ),
    )
    query_local = query_six.reshape(block_len, heads_here, HEAD_DIM)
    keys_local = keys_six.reshape(block_len, heads_here, HEAD_DIM)
    values_local = values_six.reshape(block_len, heads_here, HEAD_DIM)

    def key_token(positions):
        source_dev = positions // block_len
        within = positions % block_len
        sub_source = within // (n_head * row_count)
        head_source = within // row_count % n_head
        offset = within % row_count
        return ((source_dev * n_head + head_source) * n_sub + sub_source) * row_count + offset

    query_tokens = key_token(blk_index * block_len + jnp.arange(block_len, dtype=jnp.int32))
    first_head = (head_index * n_sub + sub_index) * heads_here
    listed_rows = query_rows(block_lists, first_head, heads_here, query_tokens)
    fold_step = make_step(query_local, listed_rows, key_token, block_len, tile_total)
    state_end = fold_step(
        start_state(heads_here, block_len),
        (
            lax.all_gather(keys_local, "blk", axis=0, tiled=True),
            lax.all_gather(values_local, "blk", axis=0, tiled=True),
        ),
        jnp.int32(0),
    )
    result_rows = normalize(state_end)
    attended = result_rows.reshape(n_sub, n_head, row_count, 1, 1, heads_here * HEAD_DIM)
    returned = lax.all_to_all(
        lax.all_to_all(attended, "head", split_axis=1, concat_axis=3, tiled=True),
        "sub",
        split_axis=0,
        concat_axis=4,
        tiled=True,
    )
    return returned.reshape(row_count, col_count)


def solution(mesh):
    in_specs = (
        P(("grp", "blk", "head", "sub"), None),
        P(("grp", "blk", "head", "sub"), None),
        P(("grp", "blk", "head", "sub"), None),
        P(),
    )
    out_specs = P(("grp", "blk", "head", "sub"), None)
    return jax.shard_map(
        per_device, mesh=mesh, in_specs=in_specs, out_specs=out_specs, check_vma=False
    )
```

profile of v0, /device:TPU:25, one launch (start us, length us, event | category | flops | bytes accessed | tf_op | source)
XLA Modules:
  0.0 297.4 jit_solution(9363083604332328994)
XLA Ops:
  9.3 15.4 %all_to_all.132 = bf16[1,1,128,2,2,1024]{2,4,5,1,0,3:T(2,128)(2,1)S(1)} all-to-all(bf16[1,1,128,2,2,1024]{2,4,5,1,0,3:T(2,128)(2,1)S(1)} %copy.75), channel_id=1, replica_groups=mesh['grp'=2,'blk'=4,'head'=2,'sub'=2] {'head'}, dimensions={3} | all-to-all | bytes 2097152 | tf_op jit(solution)/shard_map/all_to_all | solution.py:119
  25.7 6.0 %all_to_all.133 = bf16[1,2,128,1,2,1024]{2,1,5,3,0,4:T(2,128)(2,1)S(1)} all-to-all(bf16[1,2,128,1,2,1024]{2,1,5,3,0,4:T(2,128)(2,1)S(1)} %copy.76), channel_id=1, replica_groups=mesh['grp'=2,'blk'=4,'head'=2,'sub'=2] {'sub'}, dimensions={4} | all-to-all | bytes 2097152 | tf_op jit(solution)/shard_map/all_to_all | solution.py:118
  35.1 15.9 %all_to_all.134 = bf16[1,1,128,2,2,1024]{5,2,4,1,0,3:T(8,128)(2,1)S(1)} all-to-all(bf16[1,1,128,2,2,1024]{5,2,4,1,0,3:T(8,128)(2,1)S(1)} %copy.69), channel_id=1, replica_groups=mesh['grp'=2,'blk'=4,'head'=2,'sub'=2] {'head'}, dimensions={3} | all-to-all | bytes 2097152 | tf_op jit(solution)/shard_map/all_to_all | solution.py:112
  51.0 5.5 %all_to_all.135 = bf16[1,2,128,1,2,1024]{5,2,1,3,0,4:T(8,128)(2,1)S(1)} all-to-all(bf16[1,2,128,1,2,1024]{5,2,1,3,0,4:T(8,128)(2,1)S(1)} %copy.70), channel_id=1, replica_groups=mesh['grp'=2,'blk'=4,'head'=2,'sub'=2] {'sub'}, dimensions={4} | all-to-all | bytes 2097152 | tf_op jit(solution)/shard_map/all_to_all | solution.py:111
  59.7 3.6 %all-to-all-start.2 = ((bf16[1,1,128,2,2,1024]{5,2,4,1,0,3:T(8,128)(2,1)}), bf16[1,1,128,2,2,1024]{5,2,4,1,0,3:T(8,128)(2,1)S(1)}, u32[]{:S(2)}, u32[]{:S(2)}) async-start(bf16[1,1,128,2,2,1024]{5,2,4,1,0,3:T(8,128)(2,1)} %copy.72), calls=%async_computation.2 | async-start | bytes 2097152 | tf_op jit(solution)/shard_map/all_to_all | solution.py:105
  64.1 12.7 %all-to-all-done.2 = bf16[1,1,128,2,2,1024]{5,2,4,1,0,3:T(8,128)(2,1)S(1)} async-done(((bf16[1,1,128,2,2,1024]{5,2,4,1,0,3:T(8,128)(2,1)}), bf16[1,1,128,2,2,1024]{5,2,4,1,0,3:T(8,128)(2,1)S(1)}, u32[]{:S(2)}, u32[]{:S(2)}) %all-to-all-start.2) | async-done | bytes 1048608 | tf_op jit(solution)/shard_map/all_to_all | solution.py:105
  76.8 5.4 %all_to_all.136 = bf16[1,2,128,1,2,1024]{5,2,1,3,0,4:T(8,128)(2,1)S(1)} all-to-all(bf16[1,2,128,1,2,1024]{5,2,1,3,0,4:T(8,128)(2,1)S(1)} %copy.73), channel_id=1, replica_groups=mesh['grp'=2,'blk'=4,'head'=2,'sub'=2] {'sub'}, dimensions={4} | all-to-all | bytes 2097152 | tf_op jit(solution)/shard_map/all_to_all | solution.py:104
  83.6 28.2 %all-gather.5.cloned.1.call-done = bf16[2048,8,128]{2,1,0:T(8,128)(2,1)} async-done(((bf16[512,8,128]{2,1,0:T(8,128)(2,1)}), bf16[2048,8,128]{2,1,0:T(8,128)(2,1)}) %all-gather.5.cloned.1.call-update) | async-done | bytes 4194320 | tf_op jit(solution)/shard_map/all_gather | solution.py:146
  111.9 80.8 %all-gather.3.cloned.1.call-done = bf16[2048,8,128]{2,1,0:T(8,128)(2,1)} async-done(((bf16[512,8,128]{2,1,0:T(8,128)(2,1)}), bf16[2048,8,128]{2,1,0:T(8,128)(2,1)}) %all-gather.3.cloned.1.call-update) | async-done | bytes 4194320 | tf_op jit(solution)/shard_map/all_gather | solution.py:145
  192.7 69.2 %while.21 = (s32[]{:T(128)}, f32[8,512]{1,0:T(8,128)S(1)}, f32[8,512]{1,0:T(8,128)S(1)}, f32[512,8,128]{0,2,1:T(8,128)}, bf16[8,512,16]{1,2,0:T(8,128)(2,1)S(1)}...) while((s32[]{:T(128)}, f32[8,512]{1,0:T(8,128)S(1)}, ...), condition=%wide.region_4.5_spmd.clone, body=%wide.region_1.4_spmd.clone.sunk | while | flops 1167663616 | bytes 110498048 | solution.py:72
  194.4 2.5 fusion.73
  196.9 2.6 fusion.74
  200.1 7.1 %bitcast_add_fusion.2 = f32[512,8,128]{0,2,1:T(8,128)} fusion(f32[512,8,128]{0,2,1:T(8,128)} %get-tuple-element.444, f32[8,512,512]{2,1,0:T(8,128)} %copy-done.1, pred[512,8,512]{2,0,1:T(32,128)(4,1)S(1)} %get-tuple-element.426, f32[8,512]{1,0:T(8,128)S(1)} %get-tuple-element.454, bf16[512,8,128]{2,1,0:T(8,128)(2,1)S(1)} %get-tuple-element.427, ...), kind=kOutput, calls=%fused_computation.13.clone.1 | convolution fusion | flops 546832384 | bytes 15761409 | tf_op jit(solution)/shard_map/while/body/eval_jaxpr/hqk,khd->qhd/dot_general | solution.py:35
  211.2 2.5 fusion.73
  213.8 2.6 fusion.74
  217.0 7.7 %bitcast_add_fusion.2 = f32[512,8,128]{0,2,1:T(8,128)} fusion(f32[512,8,128]{0,2,1:T(8,128)} %get-tuple-element.444, f32[8,512,512]{2,1,0:T(8,128)} %copy-done.1, pred[512,8,512]{2,0,1:T(32,128)(4,1)S(1)} %get-tuple-element.426, f32[8,512]{1,0:T(8,128)S(1)} %get-tuple-element.454, bf16[512,8,128]{2,1,0:T(8,128)(2,1)S(1)} %get-tuple-element.427, ...), kind=kOutput, calls=%fused_computation.13.clone.1 | convolution fusion | flops 546832384 | bytes 15761409 | tf_op jit(solution)/shard_map/while/body/eval_jaxpr/hqk,khd->qhd/dot_general | solution.py:35
  228.7 2.5 fusion.73
  231.2 2.6 fusion.74
  234.4 7.7 %bitcast_add_fusion.2 = f32[512,8,128]{0,2,1:T(8,128)} fusion(f32[512,8,128]{0,2,1:T(8,128)} %get-tuple-element.444, f32[8,512,512]{2,1,0:T(8,128)} %copy-done.1, pred[512,8,512]{2,0,1:T(32,128)(4,1)S(1)} %get-tuple-element.426, f32[8,512]{1,0:T(8,128)S(1)} %get-tuple-element.454, bf16[512,8,128]{2,1,0:T(8,128)(2,1)S(1)} %get-tuple-element.427, ...), kind=kOutput, calls=%fused_computation.13.clone.1 | convolution fusion | flops 546832384 | bytes 15761409 | tf_op jit(solution)/shard_map/while/body/eval_jaxpr/hqk,khd->qhd/dot_general | solution.py:35
  246.1 2.5 fusion.73
  248.7 2.6 fusion.74
  251.9 7.7 %bitcast_add_fusion.2 = f32[512,8,128]{0,2,1:T(8,128)} fusion(f32[512,8,128]{0,2,1:T(8,128)} %get-tuple-element.444, f32[8,512,512]{2,1,0:T(8,128)} %copy-done.1, pred[512,8,512]{2,0,1:T(32,128)(4,1)S(1)} %get-tuple-element.426, f32[8,512]{1,0:T(8,128)S(1)} %get-tuple-element.454, bf16[512,8,128]{2,1,0:T(8,128)(2,1)S(1)} %get-tuple-element.427, ...), kind=kOutput, calls=%fused_computation.13.clone.1 | convolution fusion | flops 546832384 | bytes 15761409 | tf_op jit(solution)/shard_map/while/body/eval_jaxpr/hqk,khd->qhd/dot_general | solution.py:35
  266.0 15.4 %all_to_all.137 = bf16[2,2,128,1,1,1024]{5,0,2,4,3,1:T(2,128)(2,1)S(1)} all-to-all(bf16[2,2,128,1,1,1024]{5,0,2,4,3,1:T(2,128)(2,1)S(1)} %copy.82), channel_id=1, replica_groups=mesh['grp'=2,'blk'=4,'head'=2,'sub'=2] {'head'}, dimensions={1} | all-to-all | bytes 2097152 | tf_op jit(solution)/shard_map/all_to_all | solution.py:153
  282.4 5.8 %all_to_all.138 = bf16[2,1,128,2,1,1024]{5,3,2,4,1,0:T(2,128)(2,1)S(1)} all-to-all(bf16[2,1,128,2,1,1024]{5,3,2,4,1,0:T(2,128)(2,1)S(1)} %copy.83), channel_id=1, replica_groups=mesh['grp'=2,'blk'=4,'head'=2,'sub'=2] {'sub'}, dimensions={0} | all-to-all | bytes 2097152 | tf_op jit(solution)/shard_map/all_to_all | solution.py:152
  (90 shorter events, 38.4 us)
Async XLA Ops:
  6.5 56.8 %copy-start = (s32[32,16,8]{0,2,1:T(8,128)S(1)}, s32[32,16,8]{0,2,1:T(8,128)}, u32[]{:S(2)}) copy-start(s32[32,16,8]{0,2,1:T(8,128)} %param.9) | copy-start | bytes 49156
  6.5 105.3 %all-gather.5.cloned.1.call-start = ((), (), s32[]{:S(2)}) async-start(), calls=%async_computation.9 | async-start | bytes 5242880 | tf_op jit(solution)/shard_map/all_gather | solution.py:146
  25.7 8.1 %copy-start.2 = (bf16[128,4096]{1,0:T(8,128)(2,1)S(1)}, bf16[128,4096]{1,0:T(8,128)(2,1)}, u32[]{:S(2)}) copy-start(bf16[128,4096]{1,0:T(8,128)(2,1)} %param.7) | copy-start | bytes 3145732
  33.8 158.9 %all-gather.3.cloned.1.call-start = ((), (), s32[]{:S(2)}) async-start(), calls=%async_computation.8 | async-start | bytes 5242880 | tf_op jit(solution)/shard_map/all_gather | solution.py:145
  50.9 6.8 %copy-start.3 = (bf16[128,4096]{1,0:T(8,128)(2,1)S(1)}, bf16[128,4096]{1,0:T(8,128)(2,1)}, u32[]{:S(2)}) copy-start(bf16[128,4096]{1,0:T(8,128)(2,1)} %param.6) | copy-start | bytes 3145732
  59.7 17.0 %all-to-all-start.2 = ((bf16[1,1,128,2,2,1024]{5,2,4,1,0,3:T(8,128)(2,1)}), bf16[1,1,128,2,2,1024]{5,2,4,1,0,3:T(8,128)(2,1)S(1)}, u32[]{:S(2)}, u32[]{:S(2)}) async-start(bf16[1,1,128,2,2,1024]{5,2,4,1,0,3:T(8,128)(2,1)} %copy.72), calls=%async_computation.2 | async-start | bytes 2097152 | tf_op jit(solution)/shard_map/all_to_all | solution.py:105
  196.8 3.2 %copy-start.1 = (f32[8,512,512]{2,1,0:T(8,128)}, f32[8,512,512]{2,1,0:T(8,128)S(1)}, u32[]{:S(2)}) copy-start(f32[8,512,512]{2,1,0:T(8,128)S(1)} %fusion.73) | copy-start | bytes 25165828 | tf_op jit(solution)/shard_map/while
  200.1 7.2 %slice-start = ((s8[8388608]{0:T(1024)(128)(4,1)}), s8[4194304]{0:T(1024)(128)(4,1)S(1)}, s32[]{:S(2)}) async-start(s8[8388608]{0:T(1024)(128)(4,1)} %bitcast.120), calls=%async_computation.10 | async-start | bytes 8388608 | tf_op jit(solution)/shard_map/while
  200.1 7.2 %slice-start.1 = ((s8[8388608]{0:T(1024)(128)(4,1)}), s8[4194304]{0:T(1024)(128)(4,1)S(1)}, s32[]{:S(2)}) async-start(s8[8388608]{0:T(1024)(128)(4,1)} %bitcast.120), calls=%async_computation.11 | async-start | bytes 8388608 | tf_op jit(solution)/shard_map/while
  213.7 3.2 %copy-start.1 = (f32[8,512,512]{2,1,0:T(8,128)}, f32[8,512,512]{2,1,0:T(8,128)S(1)}, u32[]{:S(2)}) copy-start(f32[8,512,512]{2,1,0:T(8,128)S(1)} %fusion.73) | copy-start | bytes 25165828 | tf_op jit(solution)/shard_map/while
  216.9 7.8 %slice-start = ((s8[8388608]{0:T(1024)(128)(4,1)}), s8[4194304]{0:T(1024)(128)(4,1)S(1)}, s32[]{:S(2)}) async-start(s8[8388608]{0:T(1024)(128)(4,1)} %bitcast.120), calls=%async_computation.10 | async-start | bytes 8388608 | tf_op jit(solution)/shard_map/while
  217.0 7.8 %slice-start.1 = ((s8[8388608]{0:T(1024)(128)(4,1)}), s8[4194304]{0:T(1024)(128)(4,1)S(1)}, s32[]{:S(2)}) async-start(s8[8388608]{0:T(1024)(128)(4,1)} %bitcast.120), calls=%async_computation.11 | async-start | bytes 8388608 | tf_op jit(solution)/shard_map/while
  231.2 3.2 %copy-start.1 = (f32[8,512,512]{2,1,0:T(8,128)}, f32[8,512,512]{2,1,0:T(8,128)S(1)}, u32[]{:S(2)}) copy-start(f32[8,512,512]{2,1,0:T(8,128)S(1)} %fusion.73) | copy-start | bytes 25165828 | tf_op jit(solution)/shard_map/while
  234.4 7.8 %slice-start = ((s8[8388608]{0:T(1024)(128)(4,1)}), s8[4194304]{0:T(1024)(128)(4,1)S(1)}, s32[]{:S(2)}) async-start(s8[8388608]{0:T(1024)(128)(4,1)} %bitcast.120), calls=%async_computation.10 | async-start | bytes 8388608 | tf_op jit(solution)/shard_map/while
  234.4 7.8 %slice-start.1 = ((s8[8388608]{0:T(1024)(128)(4,1)}), s8[4194304]{0:T(1024)(128)(4,1)S(1)}, s32[]{:S(2)}) async-start(s8[8388608]{0:T(1024)(128)(4,1)} %bitcast.120), calls=%async_computation.11 | async-start | bytes 8388608 | tf_op jit(solution)/shard_map/while
  248.6 3.2 %copy-start.1 = (f32[8,512,512]{2,1,0:T(8,128)}, f32[8,512,512]{2,1,0:T(8,128)S(1)}, u32[]{:S(2)}) copy-start(f32[8,512,512]{2,1,0:T(8,128)S(1)} %fusion.73) | copy-start | bytes 25165828 | tf_op jit(solution)/shard_map/while
  251.9 7.8 %slice-start = ((s8[8388608]{0:T(1024)(128)(4,1)}), s8[4194304]{0:T(1024)(128)(4,1)S(1)}, s32[]{:S(2)}) async-start(s8[8388608]{0:T(1024)(128)(4,1)} %bitcast.120), calls=%async_computation.10 | async-start | bytes 8388608 | tf_op jit(solution)/shard_map/while
  251.9 7.8 %slice-start.1 = ((s8[8388608]{0:T(1024)(128)(4,1)}), s8[4194304]{0:T(1024)(128)(4,1)S(1)}, s32[]{:S(2)}) async-start(s8[8388608]{0:T(1024)(128)(4,1)} %bitcast.120), calls=%async_computation.11 | async-start | bytes 8388608 | tf_op jit(solution)/shard_map/while
Sparse Core Ops, SparseCore 0:
  33.9 77.8 all-gather.4
  113.4 79.2 all-gather.2
where the time goes:
time: 302 us; the launch traced here: 297 us
  waiting for transfers between devices  122 us (40%)
  blocking collectives  69.3 us (23%)
  matrix products  50.8 us (17%)
  local copies, waits for them, and re-layouts  26.8 us (9%)
  between operations  13.6 us (5%)
  other arithmetic  11.3 us (4%)
  starting transfers between devices  3.63 us (1%)
    all_gather x1, waiting for transfers between devices, per_device(): lax.all_gather(keys_local, 'blk', axis=0, tiled=True)  80.8 us
    dot_general x4, matrix products, attend_block(): jnp.einsum('hqk,khd->qhd', weights.astype(jnp.bfloat16), value_block, pre...  30.4 us
    all_gather x1, waiting for transfers between devices, per_device(): lax.all_gather(values_local, 'blk', axis=0, tiled=True)  28.2 us
    all_to_all x1, blocking collectives, per_device(): lax.all_to_all(inward(keys), 'head', split_axis=3, concat_axis=1, tiled=T...  15.9 us
    all_to_all x1, blocking collectives, per_device(): lax.all_to_all(attended, 'head', split_axis=1, concat_axis=3, tiled=True)  15.4 us
    all_to_all x1, blocking collectives, per_device(): lax.all_to_all(inward(values), 'head', split_axis=3, concat_axis=1, tiled...  15.4 us
    all_to_all x1, waiting for transfers between devices, per_device(): lax.all_to_all(inward(queries), 'head', split_axis=3, concat_axis=1, tile...  12.7 us
    dot_general x4, matrix products, one_block(): jnp.einsum('hqj,jk->hqk', listed_rows, key_onehot, preferred_element_type...  10.3 us
  transfers between devices with their start and end apart: 3, of which 3 were waited for; matrix products, arithmetic and copies ran while one was open for 2% of the time, Pallas kernels for 0%

commit v1 on v0

--- a/solution.py
+++ b/solution.py
@@ -1,8 +1,11 @@
+import functools
 import math
 
 import jax
 import jax.numpy as jnp
 from jax import lax
+from jax.experimental import pallas as pl
+from jax.experimental.pallas import tpu as pltpu
 from jax.sharding import PartitionSpec as P
 
 HEADS = 32
@@ -159,7 +162,186 @@
     return returned.reshape(row_count, col_count)
 
 
+def attend_tile(lists, buf, tile_out, h, i):
+    score_scale = 1.0 / math.sqrt(HEAD_DIM)
+    entries = lists.shape[2]
+    query = buf[0, i]
+    ids = [lists[h, i, e] for e in range(entries)]
+    scores, top = [], None
+    for e in range(entries):
+        s = lax.dot_general(
+            query, buf[1, ids[e]], (((1,), (1,)), ((), ())), preferred_element_type=jnp.float32
+        ) * score_scale
+        scores.append(s)
+        top = s if top is None else jnp.maximum(top, s)
+    row_top = jnp.max(top, axis=1, keepdims=True)
+    total, accum = None, None
+    for e in range(entries):
+        w = jnp.exp(scores[e] - row_top)
+        if e:
+            repeat = ids[e] == ids[0]
+            for f in range(1, e):
+                repeat = jnp.logical_or(repeat, ids[e] == ids[f])
+            w = w * jnp.where(repeat, 0.0, 1.0)
+        part = jnp.dot(
+            w.astype(jnp.bfloat16), buf[2, ids[e]], preferred_element_type=jnp.float32
+        )
+        total = w if total is None else total + w
+        accum = part if accum is None else accum + part
+    row_total = jnp.sum(total, axis=1, keepdims=True)
+    tile_out[h, i] = (accum / row_total).astype(jnp.bfloat16)
+
+
+def exchange_kernel(sizes, heads_here, q_ref, k_ref, v_ref, lists_ref, out_ref, tile_out,
+                    lists, send_sem, recv_sem, local_sem, list_sem, *bufs):
+    n_blk, n_head, n_sub = sizes
+    count = n_blk * n_head * n_sub
+    me = (lax.axis_index("blk") * n_head + lax.axis_index("head")) * n_sub + lax.axis_index("sub")
+    sources = (q_ref, k_ref, v_ref)
+
+    def coords(rank):
+        return {
+            "blk": rank // (n_head * n_sub),
+            "head": rank // n_sub % n_head,
+            "sub": rank % n_sub,
+        }
+
+    def peer(d):
+        return (me + d) % count
+
+    def columns(rank, h):
+        return pl.ds(pl.multiple_of((rank * heads_here + h) * HEAD_DIM, HEAD_DIM), HEAD_DIM)
+
+    def inward(t, h, target, sender):
+        return pltpu.make_async_remote_copy(
+            src_ref=sources[t].at[:, columns(target, h)],
+            dst_ref=bufs[h].at[t, sender],
+            send_sem=send_sem.at[t, h, target],
+            recv_sem=recv_sem.at[t, h, sender],
+            device_id=coords(target),
+            device_id_type=pl.DeviceIdType.MESH,
+        )
+
+    def outward(h, target, sender):
+        return pltpu.make_async_remote_copy(
+            src_ref=tile_out.at[h, target],
+            dst_ref=out_ref.at[:, columns(sender, h)],
+            send_sem=send_sem.at[3, h, target],
+            recv_sem=recv_sem.at[3, h, sender],
+            device_id=coords(target),
+            device_id_type=pl.DeviceIdType.MESH,
+        )
+
+    def own_in(t, h):
+        return pltpu.make_async_copy(
+            sources[t].at[:, columns(me, h)], bufs[h].at[t, me], local_sem.at[t, h]
+        )
+
+    def own_out(h):
+        return pltpu.make_async_copy(
+            tile_out.at[h, me], out_ref.at[:, columns(me, h)], local_sem.at[3, h]
+        )
+
+    own_lists = pltpu.make_async_copy(
+        lists_ref.at[pl.ds(me * heads_here, heads_here)], lists, list_sem
+    )
+    own_lists.start()
+    for h in range(heads_here):
+        for t in range(3):
+            own_in(t, h).start()
+
+    barrier = pltpu.get_barrier_semaphore()
+
+    def greet(d, carry):
+        pl.semaphore_signal(
+            barrier, inc=1, device_id=coords(peer(d)), device_id_type=pl.DeviceIdType.MESH
+        )
+        return carry
+
+    lax.fori_loop(1, count, greet, 0)
+    pl.semaphore_wait(barrier, count - 1)
+
+    for h in range(heads_here):
+        def send_in(d, carry, h=h):
+            for t in range(3):
+                inward(t, h, peer(d), me).start()
+            return carry
+
+        lax.fori_loop(1, count, send_in, 0)
+
+    own_lists.wait()
+    for h in range(heads_here):
+        for t in range(3):
+            own_in(t, h).wait()
+
+        def arrive(d, carry, h=h):
+            for t in range(3):
+                inward(t, h, me, peer(d)).wait_recv()
+            return carry
+
+        lax.fori_loop(1, count, arrive, 0)
+
+        def work(d, carry, h=h):
+            attend_tile(lists, bufs[h], tile_out, h, peer(d))
+
+            @pl.when(d > 1)
+            def _():
+                outward(h, peer(d - 1), me).start()
+
+            return carry
+
+        lax.fori_loop(1, count, work, 0)
+        attend_tile(lists, bufs[h], tile_out, h, me)
+        outward(h, peer(count - 1), me).start()
+        own_out(h).start()
+
+    for h in range(heads_here):
+        own_out(h).wait()
+
+        def finish(d, carry, h=h):
+            other = peer(d)
+            for t in range(3):
+                inward(t, h, other, me).wait_send()
+            outward(h, other, me).wait_send()
+            outward(h, me, other).wait_recv()
+            return carry
+
+        lax.fori_loop(1, count, finish, 0)
+
+
+def whole_exchange(sizes, queries, keys, values, block_lists):
+    count = sizes[0] * sizes[1] * sizes[2]
+    heads_here = HEADS // count
+    rows = queries.shape[0]
+    tiles, entries = block_lists.shape[1:]
+    any_space = pl.BlockSpec(memory_space=pl.ANY)
+    return pl.pallas_call(
+        functools.partial(exchange_kernel, sizes, heads_here),
+        out_shape=jax.ShapeDtypeStruct(queries.shape, jnp.bfloat16),
+        in_specs=[any_space] * 4,
+        out_specs=any_space,
+        scratch_shapes=[
+            pltpu.VMEM((heads_here, count, rows, HEAD_DIM), jnp.bfloat16),
+            pltpu.SMEM((heads_here, tiles, entries), jnp.int32),
+            pltpu.SemaphoreType.DMA((4, heads_here, count)),
+            pltpu.SemaphoreType.DMA((4, heads_here, count)),
+            pltpu.SemaphoreType.DMA((4, heads_here)),
+            pltpu.SemaphoreType.DMA,
+            *[pltpu.VMEM((3, count, rows, HEAD_DIM), jnp.bfloat16) for _ in range(heads_here)],
+        ],
+        compiler_params=pltpu.CompilerParams(collective_id=0, has_side_effects=True),
+    )(queries, keys, values, block_lists)
+
+
 def solution(mesh):
+    sizes = tuple(mesh.shape[axis] for axis in ("blk", "head", "sub"))
+    count = sizes[0] * sizes[1] * sizes[2]
+
+    def body(queries, keys, values, block_lists):
+        if queries.shape[0] == TILE and HEADS % count == 0:
+            return whole_exchange(sizes, queries, keys, values, block_lists)
+        return per_device(queries, keys, values, block_lists)
+
     in_specs = (
         P(("grp", "blk", "head", "sub"), None),
         P(("grp", "blk", "head", "sub"), None),
@@ -168,5 +350,5 @@
     )
     out_specs = P(("grp", "blk", "head", "sub"), None)
     return jax.shard_map(
-        per_device, mesh=mesh, in_specs=in_specs, out_specs=out_specs, check_vma=False
-    )
+        body, mesh=mesh, in_specs=in_specs, out_specs=out_specs, check_vma=False
+    )

time: 302 us -> 105 us (0.35); the launches traced: 297 us -> 105 us
  waiting for transfers between devices: 122 us -> 0 us
  Pallas kernels: 0 us -> 101 us
  blocking collectives: 69.3 us -> 0 us
  matrix products: 50.8 us -> 0 us
  local copies, waits for them, and re-layouts: 26.8 us -> 3.97 us
  between operations: 13.6 us -> 0.01 us
  other arithmetic: 11.3 us -> 0 us
  starting transfers between devices: 3.63 us -> 0 us
    all_gather x2 -> x0, waiting for transfers between devices: 109 us -> none  [the longest x1 80.8 us: per_device(): lax.all_gather(keys_local, 'blk', axis=0, tiled=True)]
    pallas_call x0 -> x1, Pallas kernels: none -> 101 us  [whole_exchange(): pl.pallas_call(functools.partial(exchange_kernel, sizes, heads_here), out...]
    all_to_all x7 -> x0, blocking collectives: 69.3 us -> none  [the longest x1 15.9 us: per_device(): lax.all_to_all(inward(keys), 'head', split_axis=3, concat_axis=1, tiled=T...]
    dot_general x13 -> x0, matrix products: 50.8 us -> none  [the longest x4 30.4 us: attend_block(): jnp.einsum('hqk,khd->qhd', weights.astype(jnp.bfloat16), value_block, pre...]
    all_to_all x1 -> x0, waiting for transfers between devices: 12.7 us -> none  [per_device(): lax.all_to_all(inward(queries), 'head', split_axis=3, concat_axis=1, tile...]
    reduce_sum x4 -> x0, other arithmetic: 8.9 us -> none  [attend_block(): total_new = total_old * factor + jnp.sum(weights, axis=2)]
    dynamic_slice x6 -> x0, local copies, waits for them, and re-layouts: 6.89 us -> none  [the longest x4 6.72 us: one_block(): lax.dynamic_slice_in_dim(value_piece, block_index * block_len, block_len, 0)]
    reshape x6 -> x0, local copies, waits for them, and re-layouts: 6.4 us -> none  [the longest x3 2.93 us: inward(): return tensor.reshape(1, 1, row_count, n_head, n_sub, heads_here * HEAD_DIM)]
  transfers between devices with their start and end apart: 3 -> 0, of which waited for: 3 -> 0; matrix products, arithmetic and copies ran while one was open for 2% -> 0% of each run, Pallas kernels for 0% -> 0%
where the time goes in v1:
time: 105 us
  Pallas kernels  101 us (96%)
  local copies, waits for them, and re-layouts  3.97 us (4%)
    pallas_call x1, Pallas kernels, whole_exchange(): pl.pallas_call(functools.partial(exchange_kernel, sizes, heads_here), out...  101 us
    unnamed x2, local copies, waits for them, and re-layouts  3.97 us

profile of v1, /device:TPU:25, one launch (start us, length us, event | category | flops | bytes accessed | tf_op | source)
XLA Modules:
  0.0 105.3 jit_solution(12825028398144826937)
XLA Ops:
  0.0 1.7 %copy.5.lists_ref = s32[32,16,8]{2,1,0:T(8,128)} copy(s32[32,16,8]{0,2,1:T(8,128)} %param.7) | data formatting | bytes 32768 | tf_op args[3]
  1.7 101.3 %shard_map.46 = bf16[128,4096]{1,0:T(8,128)(2,1)} custom-call(bf16[128,4096]{1,0:T(8,128)(2,1)} %q_ref.1, bf16[128,4096]{1,0:T(8,128)(2,1)} %k_ref.1, bf16[128,4096]{1,0:T(8,128)(2,1)} %v_ref.1, s32[32,16,8]{2,1,0:T(8,128)} %copy.5.lists_ref), custom_call_target="tpu_custom_call" | custom-call | tf_op jit(solution)/shard_map/pallas_call | solution.py:318
  103.0 2.3 %copy.7 = bf16[128,4096]{1,0:T(8,128)(2,1)} copy(bf16[128,4096]{1,0:T(8,128)(2,1)} %shard_map.46) | data formatting | bytes 2097152

commit v2 on v0

--- a/solution.py
+++ b/solution.py
@@ -1,8 +1,11 @@
+import functools
 import math
 
 import jax
 import jax.numpy as jnp
 from jax import lax
+from jax.experimental import pallas as pl
+from jax.experimental.pallas import tpu as pltpu
 from jax.sharding import PartitionSpec as P
 
 HEADS = 32
@@ -159,7 +162,417 @@
     return returned.reshape(row_count, col_count)
 
 
+NEAR_COUNTS = (0, 8, 12, 16, 20)
+
+
+def attend_tile(ids, query, buf, first):
+    score_scale = 1.0 / math.sqrt(HEAD_DIM)
+    scores, top = [], None
+    for tile in ids:
+        s = lax.dot_general(
+            query, buf[first, tile], (((1,), (1,)), ((), ())), preferred_element_type=jnp.float32
+        ) * score_scale
+        scores.append(s)
+        top = s if top is None else jnp.maximum(top, s)
+    row_top = jnp.max(top, axis=1, keepdims=True)
+    total, accum = None, None
+    for e, tile in enumerate(ids):
+        w = jnp.exp(scores[e] - row_top)
+        if e:
+            repeat = tile == ids[0]
+            for f in range(1, e):
+                repeat = jnp.logical_or(repeat, tile == ids[f])
+            w = w * jnp.where(repeat, 0.0, 1.0)
+        part = jnp.dot(
+            w.astype(jnp.bfloat16), buf[first + 1, tile], preferred_element_type=jnp.float32
+        )
+        total = w if total is None else total + w
+        accum = part if accum is None else accum + part
+    row_total = jnp.sum(total, axis=1, keepdims=True)
+    return (accum / row_total).astype(jnp.bfloat16)
+
+
+def exchange_kernel(sizes, near, stage, list_rows, landed, lists, list_sem, *scratch):
+    n_blk, n_head, n_sub = sizes
+    line_count = n_head * n_sub
+    count = n_blk * line_count
+    entries = lists.shape[2]
+    near_here = near // line_count
+    far = HEADS - near
+    far_here = -(-far // count)
+    far_in = scratch[:far_here]
+    far_out = scratch[far_here : 2 * far_here]
+    scratch = scratch[2 * far_here :]
+    near_query = scratch[:near_here]
+    near_kv = scratch[near_here : 2 * near_here]
+    near_out = scratch[2 * near_here : 3 * near_here]
+    far_send, far_recv, far_local = scratch[3 * near_here : 3 * near_here + 3]
+    if near:
+        near_send, near_recv, near_local, hop_send, hop_recv = scratch[3 * near_here + 3 :]
+
+    blk = lax.axis_index("blk")
+    line = lax.axis_index("head") * n_sub + lax.axis_index("sub")
+    me = blk * line_count + line
+
+    def remote(src, dst, send, recv, rank):
+        return pltpu.make_async_remote_copy(
+            src_ref=src,
+            dst_ref=dst,
+            send_sem=send,
+            recv_sem=recv,
+            device_id={
+                "blk": rank // line_count,
+                "head": rank // n_sub % n_head,
+                "sub": rank % n_sub,
+            },
+            device_id_type=pl.DeviceIdType.MESH,
+        )
+
+    def peer(d):
+        return (me + d) % count
+
+    def line_peer(d):
+        return (line + d) % line_count
+
+    def far_number(rank, a):
+        return a * count + rank // line_count + n_blk * (rank % line_count)
+
+    def far_inward(t, a, target, sender):
+        return remote(
+            stage.at[t, near + far_number(target, a)], far_in[a].at[t, sender],
+            far_send.at[t, a, target], far_recv.at[t, a, sender], target,
+        )
+
+    def far_outward(a, target, sender):
+        return remote(
+            far_out[a].at[target], landed.at[near + far_number(sender, a)],
+            far_send.at[3, a, target], far_recv.at[3, a, sender], target,
+        )
+
+    def far_own_in(t, a):
+        return pltpu.make_async_copy(
+            stage.at[t, near + far_number(me, a)], far_in[a].at[t, me], far_local.at[t, a]
+        )
+
+    def far_own_out(a):
+        return pltpu.make_async_copy(
+            far_out[a].at[me], landed.at[near + far_number(me, a)], far_local.at[3, a]
+        )
+
+    def if_far(rank, a, action):
+        if (a + 1) * count <= far:
+            action()
+        else:
+            pl.when(far_number(rank, a) < far)(action)
+
+    def near_slot(t, a, sender):
+        if t == 0:
+            return near_query[a].at[sender]
+        return near_kv[a].at[t - 1, line_count + sender]
+
+    def near_inward(t, a, target, sender):
+        return remote(
+            stage.at[t, a * line_count + target], near_slot(t, a, sender),
+            near_send.at[t, a, target], near_recv.at[t, a, sender], blk * line_count + target,
+        )
+
+    def near_outward(a, target, sender):
+        return remote(
+            near_out[a].at[target], landed.at[a * line_count + sender],
+            near_send.at[3, a, target], near_recv.at[3, a, sender], blk * line_count + target,
+        )
+
+    def near_own_in(t, a):
+        return pltpu.make_async_copy(
+            stage.at[t, a * line_count + line], near_slot(t, a, line), near_local.at[t, a]
+        )
+
+    def near_own_out(a):
+        return pltpu.make_async_copy(
+            near_out[a].at[line], landed.at[a * line_count + line], near_local.at[3, a]
+        )
+
+    def hop(a, direction):
+        return remote(
+            near_kv[a].at[:, pl.ds(line_count, line_count)],
+            near_kv[a].at[:, pl.ds(2 * line_count * direction, line_count)],
+            hop_send.at[a, direction], hop_recv.at[a, direction],
+            (me + line_count if direction == 0 else me + count - line_count) % count,
+        )
+
+    def each_hop(action, sending):
+        up, down = blk < n_blk - 1, blk > 0
+        pl.when(up if sending else down)(functools.partial(action, 0))
+        pl.when(down if sending else up)(functools.partial(action, 1))
+
+    barrier = pltpu.get_barrier_semaphore()
+
+    def greet(d, carry):
+        rank = peer(d)
+        pl.semaphore_signal(
+            barrier, inc=1,
+            device_id={
+                "blk": rank // line_count,
+                "head": rank // n_sub % n_head,
+                "sub": rank % n_sub,
+            },
+            device_id_type=pl.DeviceIdType.MESH,
+        )
+        return carry
+
+    lax.fori_loop(1, count, greet, 0)
+
+    def own_list(a, far_head):
+        slot = near + far_number(me, a) if far_head else a * line_count + line
+        row = near_here + a if far_head else a
+        return pltpu.make_async_copy(list_rows.at[slot], lists.at[row], list_sem.at[row])
+
+    for a in range(near_here):
+        own_list(a, False).start()
+    for a in range(far_here):
+        if_far(me, a, lambda a=a: own_list(a, True).start())
+    pl.semaphore_wait(barrier, count - 1)
+
+    for a in range(near_here):
+        def near_send_in(d, carry, a=a):
+            for t in (1, 2, 0):
+                near_inward(t, a, line_peer(d), line).start()
+            return carry
+
+        lax.fori_loop(1, line_count, near_send_in, 0)
+        for t in range(3):
+            near_own_in(t, a).start()
+
+    for a in range(far_here):
+        def far_send_in(d, carry, a=a):
+            def send(d=d):
+                for t in range(3):
+                    far_inward(t, a, peer(d), me).start()
+
+            if_far(peer(d), a, send)
+            return carry
+
+        lax.fori_loop(1, count, far_send_in, 0)
+
+        def own(a=a):
+            for t in range(3):
+                far_own_in(t, a).start()
+
+        if_far(me, a, own)
+
+    for a in range(near_here):
+        for t in range(3):
+            near_own_in(t, a).wait()
+
+        def near_arrive(d, carry, a=a):
+            for t in range(3):
+                near_inward(t, a, line, line_peer(d)).wait_recv()
+            return carry
+
+        lax.fori_loop(1, line_count, near_arrive, 0)
+        each_hop(lambda direction, a=a: hop(a, direction).start(), True)
+
+    for a in range(far_here):
+        def far_whole(a=a):
+            for t in range(3):
+                far_own_in(t, a).wait()
+
+            def far_arrive(d, carry):
+                for t in range(3):
+                    far_inward(t, a, me, peer(d)).wait_recv()
+                return carry
+
+            lax.fori_loop(1, count, far_arrive, 0)
+            own_list(a, True).wait()
+
+            def one(i):
+                ids = [lists[near_here + a, i, e] for e in range(entries)]
+                far_out[a][i] = attend_tile(ids, far_in[a][0, i], far_in[a], 1)
+
+            def work(d, carry):
+                one(peer(d))
+
+                @pl.when(d > 1)
+                def _():
+                    far_outward(a, peer(d - 1), me).start()
+
+                return carry
+
+            lax.fori_loop(1, count, work, 0)
+            one(me)
+            far_outward(a, peer(count - 1), me).start()
+            far_own_out(a).start()
+
+        if_far(me, a, far_whole)
+
+    for a in range(near_here):
+        each_hop(lambda direction, a=a: hop(a, direction).wait_recv(), False)
+        own_list(a, False).wait()
+
+        def one(i, a=a):
+            tile = blk * line_count + i
+            first = (blk - 1) * line_count
+            ids = [
+                jnp.clip(lists[a, tile, e] - first, 0, 3 * line_count - 1) for e in range(entries)
+            ]
+            near_out[a][i] = attend_tile(ids, near_query[a][i], near_kv[a], 0)
+
+        def work(d, carry, a=a, one=one):
+            one(line_peer(d))
+
+            @pl.when(d > 1)
+            def _():
+                near_outward(a, line_peer(d - 1), line).start()
+
+            return carry
+
+        lax.fori_loop(1, line_count, work, 0)
+        one(line)
+        near_outward(a, line_peer(line_count - 1), line).start()
+        near_own_out(a).start()
+
+    for a in range(far_here):
+        def finish_own(a=a):
+            far_own_out(a).wait()
+
+            def sent_back(d, carry):
+                far_outward(a, peer(d), me).wait_send()
+                return carry
+
+            lax.fori_loop(1, count, sent_back, 0)
+
+        if_far(me, a, finish_own)
+
+        def finish(d, carry, a=a):
+            def other(d=d):
+                for t in range(3):
+                    far_inward(t, a, peer(d), me).wait_send()
+                far_outward(a, me, peer(d)).wait_recv()
+
+            if_far(peer(d), a, other)
+            return carry
+
+        lax.fori_loop(1, count, finish, 0)
+
+    for a in range(near_here):
+        near_own_out(a).wait()
+        each_hop(lambda direction, a=a: hop(a, direction).wait_send(), True)
+
+        def near_finish(d, carry, a=a):
+            for t in range(3):
+                near_inward(t, a, line_peer(d), line).wait_send()
+            near_outward(a, line_peer(d), line).wait_send()
+            near_outward(a, line, line_peer(d)).wait_recv()
+            return carry
+
+        lax.fori_loop(1, line_count, near_finish, 0)
+
+
+def restore_kernel(place, landed, out_ref):
+    for h in range(HEADS):
+        out_ref[:, h * HEAD_DIM : (h + 1) * HEAD_DIM] = landed[place[h]]
+
+
+def arrange_kernel(perm, q_ref, k_ref, v_ref, lists_ref, stage, list_rows):
+    for slot in range(HEADS):
+        columns = pl.ds(pl.multiple_of(perm[slot] * HEAD_DIM, HEAD_DIM), HEAD_DIM)
+        for t, source in enumerate((q_ref, k_ref, v_ref)):
+            stage[t, slot] = source[:, columns]
+        list_rows[slot] = lists_ref[perm[slot]]
+
+
+def arrange(perm, queries, keys, values, block_lists):
+    rows, width = queries.shape
+    steps = 4
+    part = rows // steps
+    block = pl.BlockSpec((part, width), lambda i: (i, 0))
+    whole = pl.BlockSpec(block_lists.shape, lambda i: (0, 0, 0))
+    return pl.pallas_call(
+        arrange_kernel,
+        grid=(steps,),
+        out_shape=(
+            jax.ShapeDtypeStruct((3, HEADS, rows, HEAD_DIM), jnp.bfloat16),
+            jax.ShapeDtypeStruct(block_lists.shape, jnp.int32),
+        ),
+        in_specs=[pl.BlockSpec(memory_space=pltpu.SMEM), block, block, block, whole],
+        out_specs=(pl.BlockSpec((3, HEADS, part, HEAD_DIM), lambda i: (0, 0, i, 0)), whole),
+    )(perm, queries, keys, values, block_lists)
+
+
+def whole_exchange(sizes, near, collective_id, stage, list_rows, place):
+    line_count = sizes[1] * sizes[2]
+    count = sizes[0] * line_count
+    near_here = near // line_count
+    far_here = -(-(HEADS - near) // count)
+    rows = stage.shape[2]
+    block = (rows, HEAD_DIM)
+    anywhere = pl.BlockSpec(memory_space=pl.ANY)
+    smem = pl.BlockSpec(memory_space=pltpu.SMEM)
+    vmem = pl.BlockSpec(memory_space=pltpu.VMEM)
+    dma = pltpu.SemaphoreType.DMA
+    rows_here = near_here + far_here
+    scratch = [pltpu.SMEM((rows_here,) + list_rows.shape[1:], jnp.int32), dma((rows_here,))]
+    scratch += [pltpu.VMEM((3, count) + block, jnp.bfloat16)] * far_here
+    scratch += [pltpu.VMEM((count,) + block, jnp.bfloat16)] * far_here
+    scratch += [pltpu.VMEM((line_count,) + block, jnp.bfloat16)] * near_here
+    scratch += [pltpu.VMEM((2, 3 * line_count) + block, jnp.bfloat16)] * near_here
+    scratch += [pltpu.VMEM((line_count,) + block, jnp.bfloat16)] * near_here
+    scratch += [dma((4, far_here, count))] * 2 + [dma((4, far_here))]
+    if near:
+        scratch += [dma((4, near_here, line_count))] * 2 + [dma((4, near_here))]
+        scratch += [dma((near_here, 2))] * 2
+    landed = pl.pallas_call(
+        functools.partial(exchange_kernel, sizes, near),
+        out_shape=jax.ShapeDtypeStruct((HEADS,) + block, jnp.bfloat16),
+        in_specs=[anywhere, anywhere],
+        out_specs=anywhere,
+        scratch_shapes=scratch,
+        compiler_params=pltpu.CompilerParams(
+            collective_id=collective_id, has_side_effects=True
+        ),
+    )(stage, list_rows)
+    return pl.pallas_call(
+        restore_kernel,
+        out_shape=jax.ShapeDtypeStruct((rows, HEADS * HEAD_DIM), jnp.bfloat16),
+        in_specs=[smem, vmem],
+        out_specs=vmem,
+    )(place, landed)
+
+
+def head_order(block_lists, line_count):
+    heads, tiles, _ = block_lists.shape
+    frame = jnp.arange(tiles, dtype=jnp.int32)[None, :, None] // line_count
+    apart = jnp.abs(block_lists // line_count - frame)
+    is_near = jnp.max(apart, axis=(1, 2)) <= 1
+    ids = jnp.arange(heads, dtype=jnp.int32)
+    ahead = jnp.where(
+        is_near[:, None] == is_near[None, :],
+        ids[None, :] < ids[:, None],
+        is_near[None, :],
+    )
+    place = jnp.sum(ahead, axis=1, dtype=jnp.int32)
+    perm = jnp.sum(jnp.where(place[None, :] == ids[:, None], ids[None, :], 0), axis=1)
+    return perm.astype(jnp.int32), place, jnp.sum(is_near, dtype=jnp.int32)
+
+
 def solution(mesh):
+    sizes = tuple(mesh.shape[axis] for axis in ("blk", "head", "sub"))
+    line_count = sizes[1] * sizes[2]
+    count = sizes[0] * line_count
+
+    def body(queries, keys, values, block_lists):
+        if queries.shape[0] != TILE or HEADS % count or block_lists.shape[1] != count:
+            return per_device(queries, keys, values, block_lists)
+        perm, place, near_total = head_order(block_lists, line_count)
+        nears = [n for n in NEAR_COUNTS if n % line_count == 0 and n < HEADS]
+        choice = sum((near_total >= n).astype(jnp.int32) for n in nears[1:])
+        stage, list_rows = arrange(perm, queries, keys, values, block_lists)
+        branches = [
+            functools.partial(whole_exchange, sizes, n, number)
+            for number, n in enumerate(nears)
+        ]
+        return lax.switch(choice, branches, stage, list_rows, place)
+
     in_specs = (
         P(("grp", "blk", "head", "sub"), None),
         P(("grp", "blk", "head", "sub"), None),
@@ -168,5 +581,5 @@
     )
     out_specs = P(("grp", "blk", "head", "sub"), None)
     return jax.shard_map(
-        per_device, mesh=mesh, in_specs=in_specs, out_specs=out_specs, check_vma=False
-    )
+        body, mesh=mesh, in_specs=in_specs, out_specs=out_specs, check_vma=False
+    )

time: 302 us -> 99.7 us (0.33)
  waiting for transfers between devices: 122 us -> 0 us
  Pallas kernels: 0 us -> 89.8 us
  blocking collectives: 69.3 us -> 0 us
  matrix products: 50.8 us -> 0 us
  local copies, waits for them, and re-layouts: 26.8 us -> 2.65 us
  between operations: 13.6 us -> 2.63 us
  other arithmetic: 11.3 us -> 2.48 us
  starting transfers between devices: 3.63 us -> 0 us
    all_gather x2 -> x0, waiting for transfers between devices: 109 us -> none  [the longest x1 80.8 us: per_device(): lax.all_gather(keys_local, 'blk', axis=0, tiled=True)]
    pallas_call x0 -> x3, Pallas kernels: none -> 89.8 us  [the longest x1 84.8 us: whole_exchange(): pl.pallas_call(functools.partial(exchange_kernel, sizes, near), out_shape...]
    all_to_all x7 -> x0, blocking collectives: 69.3 us -> none  [the longest x1 15.9 us: per_device(): lax.all_to_all(inward(keys), 'head', split_axis=3, concat_axis=1, tiled=T...]
    dot_general x13 -> x0, matrix products: 50.8 us -> none  [the longest x4 30.4 us: attend_block(): jnp.einsum('hqk,khd->qhd', weights.astype(jnp.bfloat16), value_block, pre...]
    all_to_all x1 -> x0, waiting for transfers between devices: 12.7 us -> none  [per_device(): lax.all_to_all(inward(queries), 'head', split_axis=3, concat_axis=1, tile...]
    reduce_sum x4 -> x3, other arithmetic: 8.9 us -> 1.53 us  [the longest x1 0.71 us: head_order(): jnp.sum(jnp.where(place[None, :] == ids[:, None], ids[None, :], 0), axis=1)]
    dynamic_slice x6 -> x0, local copies, waits for them, and re-layouts: 6.89 us -> none  [the longest x4 6.72 us: one_block(): lax.dynamic_slice_in_dim(value_piece, block_index * block_len, block_len, 0)]
    reshape x6 -> x0, local copies, waits for them, and re-layouts: 6.4 us -> none  [the longest x3 2.93 us: inward(): return tensor.reshape(1, 1, row_count, n_head, n_sub, heads_here * HEAD_DIM)]
  transfers between devices with their start and end apart: 3 -> 0, of which waited for: 3 -> 0; matrix products, arithmetic and copies ran while one was open for 2% -> 0% of each run, Pallas kernels for 0% -> 0%
where the time goes in v2:
time: 99.7 us; the launch traced here: 98.1 us
  Pallas kernels  89.8 us (90%)
  local copies, waits for them, and re-layouts  2.65 us (3%)
  between operations  2.63 us (3%)
  other arithmetic  2.48 us (2%)
    pallas_call x1, Pallas kernels, whole_exchange(): pl.pallas_call(functools.partial(exchange_kernel, sizes, near), out_shape...  84.8 us
    pallas_call x1, Pallas kernels, arrange(): pl.pallas_call(arrange_kernel, grid=(steps,), out_shape=(jax.ShapeDtypeSt...  3.46 us
    unnamed x3, local copies, waits for them, and re-layouts  2.65 us

profile of v2, /device:TPU:25, one launch (start us, length us, event | category | flops | bytes accessed | tf_op | source)
XLA Modules:
  0.0 98.1 jit_solution(5791712665654906231)
XLA Ops:
  0.0 0.9 fusion.3
  0.9 0.6 convert_reduce_fusion.1
  4.2 0.2 convert_reduce_fusion
  4.4 0.7 select_reduce_fusion.perm
  5.1 1.7 %copy.11.lists_ref = s32[32,16,8]{2,1,0:T(8,128)} copy(s32[32,16,8]{0,2,1:T(8,128)} %param.12) | data formatting | bytes 32768 | tf_op args[3]
  6.8 3.5 %shard_map.51 = (bf16[3,32,128,128]{3,2,1,0:T(8,128)(2,1)S(1)}, s32[32,16,8]{2,1,0:T(8,128)S(1)}) custom-call(s32[32]{0:T(128)} %select_reduce_fusion.perm, bf16[128,4096]{1,0:T(8,128)(2,1)} %q_ref.1, bf16[128,4096]{1,0:T(8,128)(2,1)} %k_ref.1, bf16[128,4096]{1,0:T(8,128)(2,1)} %v_ref.1, s32[32,16,8]{2,1,0:T(8,128)} %copy.11.lists_ref), custom_call_target="tpu_custom_call" | custom-call | tf_op jit(solution)/shard_map/pallas_call | solution.py:490
  10.2 86.8 %conditional.1 = (bf16[128,4096]{1,0:T(8,128)(2,1)S(1)}) conditional(s32[]{:T(128)} %clamp.3, (bf16[3,32,128,128]{3,2,1,0:T(8,128)(2,1)S(1)}, s32[32,16,8]{2,1,0:T(8,128)S(1)}, s32[32]{0:T(128)S(1)}) %tuple.20, (bf16[3,32,128,128]{3,2,1,0:T(8,128)(2,1)S(1)}, s32[32,16,8]{2,1,0:T(8,128)S(1)}, ...), branch_computations={%region_4.5_spmd, %region_5.6_spmd, %region_6.7_spmd, %region_7.8_... | conditional | bytes 8 | solution.py:574
  10.3 84.8 %branch_2_fun.2.landed = bf16[32,128,128]{2,1,0:T(8,128)(2,1)} custom-call(bf16[3,32,128,128]{3,2,1,0:T(8,128)(2,1)S(1)} %get-tuple-element.48.stage, s32[32,16,8]{2,1,0:T(8,128)S(1)} %get-tuple-element.49.list_rows), custom_call_target="tpu_custom_call" | custom-call | tf_op jit(solution)/shard_map/cond/branch_2_fun/pallas_call | solution.py:524
  95.1 1.5 %branch_2_fun.3 = bf16[128,4096]{1,0:T(8,128)(2,1)S(1)} custom-call(s32[32]{0:T(128)S(1)} %get-tuple-element.47.place, bf16[32,128,128]{2,1,0:T(8,128)(2,1)} %branch_2_fun.2.landed), custom_call_target="tpu_custom_call" | custom-call | tf_op jit(solution)/shard_map/cond/branch_2_fun/pallas_call | solution.py:534
  97.1 0.0 copy-start
  97.1 1.0 copy-done
  (2 shorter events, 0.0 us)
Async XLA Ops:
  97.1 1.0 copy-start
